TPU v7x, 256 devices: a whole 4x4x8 slice. The times are simulated.
256 devices in a mesh: cam: 8 (over x, core), clip: 32 (over y, z).
Axes of the slice: x: 4, y: 4, z: 8, core: 2. Of those that a mesh axis runs over, the one named last changes fastest.
Arguments:
- tokens: bfloat16 [64, 8, 256, 1024], P('clip', 'cam'), may hold values from -6 to 6
- w_query: bfloat16 [1024, 1024], replicated, may hold values from -0.1875 to 0.1875
- w_key: bfloat16 [1024, 1024], replicated, may hold values from -0.1875 to 0.1875
- w_value: bfloat16 [1024, 1024], replicated, may hold values from -0.1875 to 0.1875
- w_proj: bfloat16 [1024, 256], replicated, may hold values from -0.1875 to 0.1875
- prototypes: bfloat16 [256, 65536], P(None, ('cam', 'clip')), may hold values from -6 to 6
Outputs:
- codes: float32 [64, 65536], P(None, ('cam', 'clip'))
- prototype_gradient: float32 [256, 65536], P(None, ('cam', 'clip'))
- grad_proj: float32 [1024, 256], P('clip')
- grad_value: float32 [1024, 1024], P('clip', 'cam')
All inputs are finite; a program needn't handle non-finite values.
Results may differ from a plain program's by a relative error of at most 0.015.
Values may be sent and summed in bfloat16 or wider, within the bound.
A program may use at most 128 MiB of HBM per device.

v0:
```python
import jax
import jax.numpy as jnp
from jax import lax
from jax.sharding import PartitionSpec as P

D = 1024
HD = 64
PROTOS = 65536
TOK = 256
ITERS = 3
H = 16
SINK_EPS = 0.05
SOFTMAX_TEMP = 0.1
NORM_EPS = 1e-06
heads_per_group = 4


def column_sums(query_rows, key_rows, total):
    scores = jnp.einsum(
        "ihe,jhe->hij", query_rows, key_rows, preferred_element_type=jnp.float32
    ) * HD ** (-0.5)
    exponent_values = jnp.exp(scores)
    probs = exponent_values / jnp.sum(exponent_values, axis=2, keepdims=True)
    return jnp.sum(probs, axis=1) / total


def camera_block(query_clip, key_clip, total):
    tokens_here = query_clip.shape[0]
    width = heads_per_group * HD
    parts = []
    for group in range(H // heads_per_group):
        query_group = query_clip[:, group * width : (group + 1) * width].reshape(
            tokens_here, heads_per_group, HD
        )
        key_group = key_clip[:, group * width : (group + 1) * width].reshape(
            total, heads_per_group, HD
        )
        parts.append(column_sums(query_group, key_group, total))
    return jnp.concatenate(parts, axis=0)


def local(tokens, w_query, w_key, w_value, w_proj, prototypes):
    clips = tokens.shape[0]
    own = tokens.reshape(clips, TOK, D)
    query_vectors = jnp.einsum(
        "ctd,de->cte", own, w_query, preferred_element_type=jnp.float32
    ).astype(jnp.bfloat16)
    key_rows = jnp.einsum("ctd,de->cte", own, w_key, preferred_element_type=jnp.float32).astype(
        jnp.bfloat16
    )
    collected_rows = lax.all_gather(key_rows.reshape(clips, 1, TOK, D), "cam", axis=1, tiled=True)
    cameras = collected_rows.shape[1]
    total = cameras * TOK

    def per_clip(clip_pair):
        return camera_block(clip_pair[0], clip_pair[1], total)

    partial_sums = lax.map(per_clip, (query_vectors, collected_rows.reshape(clips, total, D)))
    weights = lax.psum_scatter(
        partial_sums.reshape(clips, H, cameras, TOK), "cam", scatter_dimension=2, tiled=True
    )
    weights = weights.reshape(clips, H, TOK).astype(jnp.bfloat16)
    mixture = jnp.einsum("chj,cjd->chd", weights, own, preferred_element_type=jnp.float32).astype(
        jnp.bfloat16
    )
    head_out = jnp.einsum(
        "chd,dhe->che", mixture, w_value.reshape(D, H, HD), preferred_element_type=jnp.float32
    )
    pooled = lax.psum(head_out.reshape(clips, D), "cam").astype(jnp.bfloat16)
    share_rows = D // lax.axis_size("clip")
    embed = jnp.dot(pooled, w_proj, preferred_element_type=jnp.float32)
    embed_norm = jnp.sqrt(jnp.sum(embed * embed, axis=1, keepdims=True) + NORM_EPS)
    unit = embed / embed_norm
    unit_b = unit.astype(jnp.bfloat16)
    all_units = lax.all_gather(unit_b, "clip", axis=0, tiled=True)
    proto_f = prototypes.astype(jnp.float32)
    column_norm = jnp.sqrt(jnp.sum(proto_f * proto_f, axis=0, keepdims=True) + NORM_EPS)
    unit_proto = proto_f / column_norm
    proto_b = unit_proto.astype(jnp.bfloat16)
    logit_scores = jnp.dot(all_units, proto_b, preferred_element_type=jnp.float32)
    exponent_values = jnp.exp(logit_scores / SOFTMAX_TEMP)
    assign = jnp.exp(logit_scores / SINK_EPS)
    prob_total = lax.psum(jnp.sum(exponent_values, axis=1), ("cam", "clip"))
    first_step = 0
    for step in range(first_step, ITERS):
        assign = assign / jnp.sum(assign, axis=0, keepdims=True)
        row_total = lax.psum(jnp.sum(assign, axis=1), ("cam", "clip"))
        assign = assign / row_total[:, None]
    prob = exponent_values / prob_total[:, None]
    grad_logits = (PROTOS * (prob - assign)).astype(jnp.bfloat16)
    codes = PROTOS * assign
    grad_unit = lax.psum_scatter(
        jnp.dot(grad_logits, proto_b.T, preferred_element_type=jnp.float32),
        "clip",
        scatter_dimension=0,
        tiled=True,
    )
    grad_unit = lax.psum(grad_unit, "cam")
    grad_embed = (grad_unit - unit * jnp.sum(unit * grad_unit, axis=1, keepdims=True)) / embed_norm
    grad_embed_b = grad_embed.astype(jnp.bfloat16)
    grad_pooled = jnp.dot(grad_embed_b, w_proj.T, preferred_element_type=jnp.float32).astype(
        jnp.bfloat16
    )
    piece = pooled
    grad_proj = lax.psum_scatter(
        jnp.einsum("cd,ce->de", piece, grad_embed_b, preferred_element_type=jnp.float32),
        "clip",
        scatter_dimension=0,
        tiled=True,
    )
    grad_heads = grad_pooled.reshape(clips, H, HD)
    piece = lax.slice_in_dim(mixture, 0, share_rows * lax.axis_size("clip"), axis=2)
    value_rows = lax.psum_scatter(
        jnp.einsum("chd,che->dhe", piece, grad_heads, preferred_element_type=jnp.float32).reshape(
            share_rows * lax.axis_size("clip"), D
        ),
        "clip",
        scatter_dimension=0,
        tiled=True,
    )
    grad_value = lax.psum_scatter(value_rows, "cam", scatter_dimension=1, tiled=True)
    grad_unit_proto = jnp.einsum(
        "be,bk->ek", all_units, grad_logits, preferred_element_type=jnp.float32
    )
    prototype_gradient = (
        grad_unit_proto - unit_proto * jnp.sum(unit_proto * grad_unit_proto, axis=0, keepdims=True)
    ) / column_norm
    return (codes, prototype_gradient, grad_proj, grad_value)


def solution(mesh):
    in_specs = (P("clip", "cam", None, None), P(), P(), P(), P(), P(None, ("cam", "clip")))
    out_specs = (
        P(None, ("cam", "clip")),
        P(None, ("cam", "clip")),
        P("clip", None),
        P("clip", "cam"),
    )
    return jax.shard_map(local, mesh=mesh, in_specs=in_specs, out_specs=out_specs, check_vma=False)
```

profile of v0, /device:TPU:8, one launch (start us, length us, event | category | flops | bytes accessed | tf_op | source)
XLA Modules:
  0.0 1159.4 jit_solution(2229369669846176685)
XLA Ops:
  7.2 1.5 copy-done
  8.8 3.5 fusion.32
  12.4 4.0 copy.30
  16.4 3.8 fusion.29
  20.2 47.3 %all-gather.4.cloned.1.call-done = bf16[2,2048,1024]{2,1,0:T(8,128)(2,1)} async-done(((bf16[2,256,1024]{2,1,0:T(8,128)(2,1)}), bf16[2,2048,1024]{2,1,0:T(8,128)(2,1)}) %all-gather.4.cloned.1.call-update) | async-done | bytes 8388624 | tf_op jit(solution)/shard_map/all_gather | solution.py:51
  67.5 130.2 %while.10 = (s32[]{:T(128)}, f32[2,16,2048]{2,1,0:T(8,128)}, bf16[2,256,1024]{2,1,0:T(8,128)(2,1)}, bf16[2,2048,1024]{2,1,0:T(8,128)(2,1)}, s32[]{:T(128)}) while((s32[]{:T(128)}, f32[2,16,2048]{2,1,0:T(8,128)}, bf16[2,256,1024]{2,1,0:T(8,128)(2,1)}, bf16[2,2048,1024]{2,1,0:T(8,128)(2,1)}, s32[]{:T(128)}) %tuple.47), condition=%wide.region_9.10_spmd, body=%wide.region_0.9_spmd.sunk | while | flops 2181148672 | bytes 112328888 | solution.py:58
  67.5 4.6 constant_dynamic-slice_fusion.6
  72.1 6.5 copy.50
  78.6 3.8 fusion.140
  83.2 2.1 copy.49
  87.1 5.7 fusion.143
  92.9 7.5 divide_reduce_fusion.11
  100.3 4.5 fusion.144
  104.8 6.1 divide_reduce_fusion.12
  111.8 4.5 fusion.142
  116.3 5.5 divide_reduce_fusion.10
  121.8 4.5 fusion.141
  126.3 5.6 divide_reduce_fusion.9
  132.7 4.6 constant_dynamic-slice_fusion.6
  137.3 6.5 copy.50
  143.7 3.8 fusion.140
  148.4 2.1 copy.49
  152.3 5.7 fusion.143
  158.0 7.5 divide_reduce_fusion.11
  165.5 4.5 fusion.144
  169.9 6.1 divide_reduce_fusion.12
  176.9 4.5 fusion.142
  181.4 5.5 divide_reduce_fusion.10
  186.9 4.5 fusion.141
  191.4 5.6 divide_reduce_fusion.9
  197.8 1.7 copy.46
  201.4 31.9 %reduce-scatter.5.cloned.1.call-done = f32[2,16,1,256]{3,1,0,2:T(8,128)} async-done(((f32[2,16,8,256]{3,1,0,2:T(8,128)}), f32[2,16,1,256]{3,1,0,2:T(8,128)}) %reduce-scatter.5.cloned.1.call-update) | async-done | bytes 32784 | tf_op jit(solution)/shard_map/reduce_scatter | solution.py:59
  233.3 1.5 convolution_convert_fusion
  234.8 2.2 convolution_bitcast_fusion
  237.1 13.2 %psum.42 = bf16[2,1024]{1,0:T(2,128)(2,1)S(1)} all-reduce(f32[2,1024]{1,0:T(2,128)S(1)} %reshape.88), channel_id=1, replica_groups=mesh['cam'=8,'clip'=32] {'cam'}, use_global_device_ids=true, to_apply=%region_11.12 | all-reduce | flops 2048 | bytes 12288 | tf_op jit(solution)/shard_map/psum | solution.py:69
  250.3 1.3 multiply_reduce_fusion.2
  251.7 43.0 %all-gather.1 = bf16[32,2,256]{2,1,0:T(2,128)(2,1)S(1)} all-gather(bf16[1,2,256]{2,1,0:T(2,128)(2,1)S(1)} %get-tuple-element.51), channel_id=1, replica_groups=mesh['cam'=8,'clip'=32] {'clip'}, dimensions={0}, use_global_device_ids=true | all-gather | bytes 33792 | tf_op jit(solution)/shard_map/all_gather | solution.py:75
  295.1 72.7 %psum.43 = f32[64]{0:T(128)S(1)} all-reduce(f32[64]{0:T(128)S(1)} %get-tuple-element.40), channel_id=1, replica_groups=mesh['cam'=8,'clip'=32] {'cam','clip'}, use_global_device_ids=true, to_apply=%region_16.17 | all-reduce | flops 64 | bytes 512 | tf_op jit(solution)/shard_map/psum | solution.py:87
  368.0 74.3 %psum.44 = f32[64]{0:T(128)S(1)} all-reduce(f32[64]{0:T(128)S(1)} %fusion.48), channel_id=1, replica_groups=mesh['cam'=8,'clip'=32] {'cam','clip'}, use_global_device_ids=true, to_apply=%region_19.20 | all-reduce | flops 64 | bytes 512 | tf_op jit(solution)/shard_map/psum | solution.py:87
  442.6 73.4 %all-reduce.1 = (f32[64]{0:T(128)S(1)}, f32[64]{0:T(128)S(1)}) all-reduce(f32[64]{0:T(128)S(1)} %fusion.50, f32[64]{0:T(128)S(1)} %get-tuple-element.39), channel_id=1, replica_groups=mesh['cam'=8,'clip'=32] {'cam','clip'}, use_global_device_ids=true, to_apply=%region_22.23 | all-reduce | flops 128 | bytes 1024 | tf_op jit(solution)/shard_map/psum | solution.py:87
  518.8 137.5 %all-reduce.4.cloned.1.call-done = f32[64,256]{1,0:T(8,128)} async-done(((f32[64,256]{1,0:T(8,128)}), f32[64,256]{1,0:T(8,128)}) %all-reduce.4.cloned.1.call-update) | async-done | bytes 65552
  657.1 12.4 %psum.47 = f32[2,256]{1,0:T(2,128)S(1)} all-reduce(f32[2,256]{1,0:T(2,128)S(1)} %constant_dynamic-slice_fusion.2), channel_id=1, replica_groups=mesh['cam'=8,'clip'=32] {'cam'}, use_global_device_ids=true, to_apply=%region_27.28 | all-reduce | flops 512 | bytes 4096 | tf_op jit(solution)/shard_map/psum | solution.py:98
  671.0 2.7 fusion.52
  673.7 5.4 copy.35
  679.2 1.3 fusion.59
  680.6 217.1 %reduce-scatter.9.cloned.1.call-done = f32[32,1024]{1,0:T(8,128)} async-done(((f32[1024,1024]{1,0:T(8,128)}), f32[32,1024]{1,0:T(8,128)}) %reduce-scatter.9.cloned.1.call-update) | async-done | bytes 131088 | tf_op jit(solution)/shard_map/reduce_scatter | solution.py:113
  898.7 218.6 %reduce-scatter.7.cloned.1.call-done = f32[32,256]{1,0:T(8,128)} async-done(((f32[1024,256]{1,0:T(8,128)}), f32[32,256]{1,0:T(8,128)}) %reduce-scatter.7.cloned.1.call-update) | async-done | bytes 32784 | tf_op jit(solution)/shard_map/reduce_scatter | solution.py:105
  1117.3 35.2 %reduce-scatter.11.cloned.1.call-done = f32[32,128]{1,0:T(8,128)} async-done(((f32[32,1024]{1,0:T(8,128)}), f32[32,128]{1,0:T(8,128)}) %reduce-scatter.11.cloned.1.call-update) | async-done | bytes 16400 | tf_op jit(solution)/shard_map/reduce_scatter | solution.py:121
  (71 shorter events, 17.1 us)
Async XLA Ops:
  7.2 1.6 copy-start
  7.2 9.2 copy-start.5
  7.2 60.4 %all-gather.4.cloned.1.call-start = ((), (), s32[]{:S(2)}) async-start(), calls=%async_computation.8 | async-start | bytes 9437184 | tf_op jit(solution)/shard_map/all_gather | solution.py:51
  12.3 221.0 %reduce-scatter.5.cloned.1.call-start = ((), (), s32[]{:S(2)}) async-start(), calls=%async_computation.4 | async-start | bytes 294912 | tf_op jit(solution)/shard_map/reduce_scatter | solution.py:59
  67.5 450.1 %copy-start.8 = (u32[256]{0:T(256)S(1)}, u32[256]{0:T(256)}, u32[]{:S(2)}) copy-start(u32[256]{0:T(256)} %constant.40) | copy-start | bytes 3076
  78.6 3.8 copy-start.3
  86.5 0.6 copy-start.2
  126.3 5.6 copy-start.6
  132.0 0.7 copy-start.7
  143.7 3.8 copy-start.3
  151.6 0.6 copy-start.2
  191.4 5.6 copy-start.6
  197.1 0.7 copy-start.7
  199.5 456.9 %all-reduce.4.cloned.1.call-start = ((), (), s32[]{:S(2)}) async-start(), calls=%async_computation.9 | async-start | bytes 131072
  517.5 380.1 %reduce-scatter.9.cloned.1.call-start = ((), (), s32[]{:S(2)}) async-start(), calls=%async_computation.6 | async-start | bytes 4325376 | tf_op jit(solution)/shard_map/reduce_scatter | solution.py:113
  671.0 481.5 %copy-start.1 = (bf16[1024,1024]{1,0:T(8,128)(2,1)S(1)}, bf16[1024,1024]{1,0:T(8,128)(2,1)}, u32[]{:S(2)}) copy-start(bf16[1024,1024]{1,0:T(8,128)(2,1)} %param.10) | copy-start | bytes 6291460
  673.7 224.0 %copy-start.4 = (bf16[256,256]{1,0:T(8,128)(2,1)S(1)}, bf16[256,256]{1,0:T(8,128)(2,1)}, u32[]{:S(2)}) copy-start(bf16[256,256]{1,0:T(8,128)(2,1)} %param.13) | copy-start | bytes 393220
  679.1 438.2 %reduce-scatter.7.cloned.1.call-start = ((), (), s32[]{:S(2)}) async-start(), calls=%async_computation.5 | async-start | bytes 1081344 | tf_op jit(solution)/shard_map/reduce_scatter | solution.py:105
  680.5 472.0 %reduce-scatter.11.cloned.1.call-start = ((), (), s32[]{:S(2)}) async-start(), calls=%async_computation.7 | async-start | bytes 147456 | tf_op jit(solution)/shard_map/reduce_scatter | solution.py:121
Sparse Core Ops, SparseCore 0:
  12.5 55.0 all-gather.3
  199.6 33.6 reduce-scatter.4
  517.7 138.6 all-reduce.3
  679.3 218.3 reduce-scatter.8
  901.9 215.3 reduce-scatter.6
  1120.2 32.2 reduce-scatter.10
where the time goes:
time: 1160 us
  waiting for transfers between devices  688 us (59%)
  blocking collectives  289 us (25%)
  matrix products  107 us (9%)
  local copies, waits for them, and re-layouts  54.6 us (5%)
  between operations  14.9 us (1%)
    psum x3, blocking collectives, local(): row_total = lax.psum(jnp.sum(assign, axis=1), ('cam', 'clip'))  220 us
    reduce_scatter x1, waiting for transfers between devices, local(): lax.psum_scatter(jnp.einsum('cd,ce->de', piece, grad_embed_b, preferred_e...  219 us
    reduce_scatter x1, waiting for transfers between devices, local(): lax.psum_scatter(jnp.einsum('chd,che->dhe', piece, grad_heads, preferred_...  217 us
    unnamed x7, waiting for transfers between devices  138 us
    div x8, matrix products, column_sums(): probs = exponent_values / jnp.sum(exponent_values, axis=2, keepdims=True)  49.5 us
    all_gather x1, waiting for transfers between devices, local(): lax.all_gather(key_rows.reshape(clips, 1, TOK, D), 'cam', axis=1, tiled=T...  47.3 us
    all_gather x1, blocking collectives, local(): all_units = lax.all_gather(unit_b, 'clip', axis=0, tiled=True)  43 us
    dot_general x8, matrix products, column_sums(): jnp.einsum('ihe,jhe->hij', query_rows, key_rows, preferred_element_type=j...  38.4 us
  transfers between devices with their start and end apart: 6, of which 6 were waited for; matrix products, arithmetic and copies ran while one was open for 1% of the time, Pallas kernels for 0%

commit v1 on v0

--- a/solution.py
+++ b/solution.py
@@ -84,7 +84,7 @@
     first_step = 0
     for step in range(first_step, ITERS):
         assign = assign / jnp.sum(assign, axis=0, keepdims=True)
-        row_total = lax.psum(jnp.sum(assign, axis=1), ("cam", "clip"))
+        row_total = lax.psum(lax.psum(jnp.sum(assign, axis=1), "cam"), "clip")
         assign = assign / row_total[:, None]
     prob = exponent_values / prob_total[:, None]
     grad_logits = (PROTOS * (prob - assign)).astype(jnp.bfloat16)

time: 1160 us -> 1260 us (1.086)
  blocking collectives: 289 us -> 391 us
    psum x3 -> x7, blocking collectives: 220 us -> 323 us  [the longest x6 239 us: local(): row_total = lax.psum(lax.psum(jnp.sum(assign, axis=1), 'cam'), 'clip')]
where the time goes in v1:
time: 1260 us
  waiting for transfers between devices  686 us (54%)
  blocking collectives  391 us (31%)
  matrix products  107 us (8%)
  local copies, waits for them, and re-layouts  54.6 us (4%)
  between operations  14.9 us (1%)
    psum x6, blocking collectives, local(): row_total = lax.psum(lax.psum(jnp.sum(assign, axis=1), 'cam'), 'clip')  239 us
    reduce_scatter x1, waiting for transfers between devices, local(): lax.psum_scatter(jnp.einsum('cd,ce->de', piece, grad_embed_b, preferred_e...  218 us
    reduce_scatter x1, waiting for transfers between devices, local(): lax.psum_scatter(jnp.einsum('chd,che->dhe', piece, grad_heads, preferred_...  217 us
    unnamed x7, waiting for transfers between devices  136 us
    psum x1, blocking collectives, local(): prob_total = lax.psum(jnp.sum(exponent_values, axis=1), ('cam', 'clip'))  83.2 us
    div x8, matrix products, column_sums(): probs = exponent_values / jnp.sum(exponent_values, axis=2, keepdims=True)  49.5 us
    all_gather x1, waiting for transfers between devices, local(): lax.all_gather(key_rows.reshape(clips, 1, TOK, D), 'cam', axis=1, tiled=T...  47.3 us
    all_gather x1, blocking collectives, local(): all_units = lax.all_gather(unit_b, 'clip', axis=0, tiled=True)  43 us
  transfers between devices with their start and end apart: 6, of which 6 were waited for; matrix products, arithmetic and copies ran while one was open for 1% of the time, Pallas kernels for 0%

profile of v1, /device:TPU:8, one launch (start us, length us, event | category | flops | bytes accessed | tf_op | source)
XLA Modules:
  0.0 1259.8 jit_solution(10495705892645997520)
XLA Ops:
  8.8 3.5 fusion.32
  12.4 4.0 copy.30
  16.4 3.8 fusion.29
  20.2 47.3 %all-gather.4.cloned.1.call-done = bf16[2,2048,1024]{2,1,0:T(8,128)(2,1)} async-done(((bf16[2,256,1024]{2,1,0:T(8,128)(2,1)}), bf16[2,2048,1024]{2,1,0:T(8,128)(2,1)}) %all-gather.4.cloned.1.call-update) | async-done | bytes 8388624 | tf_op jit(solution)/shard_map/all_gather | solution.py:51
  67.5 130.2 %while.10 = (s32[]{:T(128)}, f32[2,16,2048]{2,1,0:T(8,128)}, bf16[2,256,1024]{2,1,0:T(8,128)(2,1)}, bf16[2,2048,1024]{2,1,0:T(8,128)(2,1)}, s32[]{:T(128)}) while((s32[]{:T(128)}, f32[2,16,2048]{2,1,0:T(8,128)}, bf16[2,256,1024]{2,1,0:T(8,128)(2,1)}, bf16[2,2048,1024]{2,1,0:T(8,128)(2,1)}, s32[]{:T(128)}) %tuple.47), condition=%wide.region_9.10_spmd, body=%wide.region_0.9_spmd.sunk | while | flops 2181148672 | bytes 112328888 | solution.py:58
  67.5 4.6 constant_dynamic-slice_fusion.6
  72.1 6.5 copy.50
  78.6 3.8 fusion.140
  83.2 2.1 copy.49
  87.1 5.7 fusion.143
  92.9 7.5 divide_reduce_fusion.11
  100.3 4.5 fusion.144
  104.8 6.1 divide_reduce_fusion.12
  111.8 4.5 fusion.142
  116.3 5.5 divide_reduce_fusion.10
  121.8 4.5 fusion.141
  126.3 5.6 divide_reduce_fusion.9
  132.7 4.6 constant_dynamic-slice_fusion.6
  137.3 6.5 copy.50
  143.7 3.8 fusion.140
  148.4 2.1 copy.49
  152.3 5.7 fusion.143
  158.0 7.5 divide_reduce_fusion.11
  165.5 4.5 fusion.144
  169.9 6.1 divide_reduce_fusion.12
  176.9 4.5 fusion.142
  181.4 5.5 divide_reduce_fusion.10
  186.9 4.5 fusion.141
  191.4 5.6 divide_reduce_fusion.9
  197.8 1.7 copy.46
  201.4 31.9 %reduce-scatter.5.cloned.1.call-done = f32[2,16,1,256]{3,1,0,2:T(8,128)} async-done(((f32[2,16,8,256]{3,1,0,2:T(8,128)}), f32[2,16,1,256]{3,1,0,2:T(8,128)}) %reduce-scatter.5.cloned.1.call-update) | async-done | bytes 32784 | tf_op jit(solution)/shard_map/reduce_scatter | solution.py:59
  234.8 2.2 convolution_bitcast_fusion
  237.1 13.2 %psum.63 = bf16[2,1024]{1,0:T(2,128)(2,1)S(1)} all-reduce(f32[2,1024]{1,0:T(2,128)S(1)} %reshape.88), channel_id=1, replica_groups=mesh['cam'=8,'clip'=32] {'cam'}, use_global_device_ids=true, to_apply=%region_11.12 | all-reduce | flops 2048 | bytes 12288 | tf_op jit(solution)/shard_map/psum | solution.py:69
  251.7 43.0 %all-gather.1 = bf16[32,2,256]{2,1,0:T(2,128)(2,1)S(1)} all-gather(bf16[1,2,256]{2,1,0:T(2,128)(2,1)S(1)} %get-tuple-element.49), channel_id=1, replica_groups=mesh['cam'=8,'clip'=32] {'clip'}, dimensions={0}, use_global_device_ids=true | all-gather | bytes 33792 | tf_op jit(solution)/shard_map/all_gather | solution.py:75
  295.1 12.4 psum.64
  307.5 62.6 %psum.65 = f32[64]{0:T(128)S(1)} all-reduce(f32[64]{0:T(128)S(1)} %psum.64), channel_id=1, replica_groups=mesh['cam'=8,'clip'=32] {'clip'}, use_global_device_ids=true, to_apply=%region_17.18 | all-reduce | flops 64 | bytes 512 | tf_op jit(solution)/shard_map/psum | solution.py:87
  370.4 12.4 psum.66
  382.8 68.0 %psum.67 = f32[64]{0:T(128)S(1)} all-reduce(f32[64]{0:T(128)S(1)} %psum.66), channel_id=1, replica_groups=mesh['cam'=8,'clip'=32] {'clip'}, use_global_device_ids=true, to_apply=%region_21.22 | all-reduce | flops 64 | bytes 512 | tf_op jit(solution)/shard_map/psum | solution.py:87
  451.1 12.4 psum.68
  463.5 71.6 %psum.69 = f32[64]{0:T(128)S(1)} all-reduce(f32[64]{0:T(128)S(1)} %psum.68), channel_id=1, replica_groups=mesh['cam'=8,'clip'=32] {'clip'}, use_global_device_ids=true, to_apply=%region_25.26 | all-reduce | flops 64 | bytes 512 | tf_op jit(solution)/shard_map/psum | solution.py:87
  535.2 83.2 %psum.70 = f32[64]{0:T(128)S(1)} all-reduce(f32[64]{0:T(128)S(1)} %get-tuple-element.39), channel_id=1, replica_groups=mesh['cam'=8,'clip'=32] {'cam','clip'}, use_global_device_ids=true, to_apply=%region_27.28 | all-reduce | flops 64 | bytes 512 | tf_op jit(solution)/shard_map/psum | solution.py:83
  621.3 135.5 %all-reduce.3.cloned.1.call-done = f32[64,256]{1,0:T(8,128)} async-done(((f32[64,256]{1,0:T(8,128)}), f32[64,256]{1,0:T(8,128)}) %all-reduce.3.cloned.1.call-update) | async-done | bytes 65552
  757.4 12.4 psum.71
  771.3 2.7 fusion.52
  774.1 5.4 copy.35
  780.9 217.1 %reduce-scatter.9.cloned.1.call-done = f32[32,1024]{1,0:T(8,128)} async-done(((f32[1024,1024]{1,0:T(8,128)}), f32[32,1024]{1,0:T(8,128)}) %reduce-scatter.9.cloned.1.call-update) | async-done | bytes 131088 | tf_op jit(solution)/shard_map/reduce_scatter | solution.py:113
  999.1 218.5 %reduce-scatter.7.cloned.1.call-done = f32[32,256]{1,0:T(8,128)} async-done(((f32[1024,256]{1,0:T(8,128)}), f32[32,256]{1,0:T(8,128)}) %reduce-scatter.7.cloned.1.call-update) | async-done | bytes 32784 | tf_op jit(solution)/shard_map/reduce_scatter | solution.py:105
  1217.6 35.4 %reduce-scatter.11.cloned.1.call-done = f32[32,128]{1,0:T(8,128)} async-done(((f32[32,1024]{1,0:T(8,128)}), f32[32,128]{1,0:T(8,128)}) %reduce-scatter.11.cloned.1.call-update) | async-done | bytes 16400 | tf_op jit(solution)/shard_map/reduce_scatter | solution.py:121
  (75 shorter events, 22.7 us)
Async XLA Ops:
  7.2 1.6 copy-start
  7.2 9.2 copy-start.5
  7.2 60.4 %all-gather.4.cloned.1.call-start = ((), (), s32[]{:S(2)}) async-start(), calls=%async_computation.8 | async-start | bytes 9437184 | tf_op jit(solution)/shard_map/all_gather | solution.py:51
  12.3 221.0 %reduce-scatter.5.cloned.1.call-start = ((), (), s32[]{:S(2)}) async-start(), calls=%async_computation.4 | async-start | bytes 294912 | tf_op jit(solution)/shard_map/reduce_scatter | solution.py:59
  67.5 552.5 %copy-start.8 = (u32[256]{0:T(256)S(1)}, u32[256]{0:T(256)}, u32[]{:S(2)}) copy-start(u32[256]{0:T(256)} %constant.40) | copy-start | bytes 3076
  78.6 3.8 copy-start.3
  86.5 0.6 copy-start.2
  126.3 5.6 copy-start.6
  132.0 0.7 copy-start.7
  143.7 3.8 copy-start.3
  151.6 0.6 copy-start.2
  191.4 5.6 copy-start.6
  197.1 0.7 copy-start.7
  199.5 557.3 %all-reduce.3.cloned.1.call-start = ((), (), s32[]{:S(2)}) async-start(), calls=%async_computation.9 | async-start | bytes 131072
  620.0 378.1 %reduce-scatter.9.cloned.1.call-start = ((), (), s32[]{:S(2)}) async-start(), calls=%async_computation.6 | async-start | bytes 4325376 | tf_op jit(solution)/shard_map/reduce_scatter | solution.py:113
  771.3 481.6 %copy-start.1 = (bf16[1024,1024]{1,0:T(8,128)(2,1)S(1)}, bf16[1024,1024]{1,0:T(8,128)(2,1)}, u32[]{:S(2)}) copy-start(bf16[1024,1024]{1,0:T(8,128)(2,1)} %param.10) | copy-start | bytes 6291460
  774.1 224.0 %copy-start.4 = (bf16[256,256]{1,0:T(8,128)(2,1)S(1)}, bf16[256,256]{1,0:T(8,128)(2,1)}, u32[]{:S(2)}) copy-start(bf16[256,256]{1,0:T(8,128)(2,1)} %param.13) | copy-start | bytes 393220
  779.5 438.1 %reduce-scatter.7.cloned.1.call-start = ((), (), s32[]{:S(2)}) async-start(), calls=%async_computation.5 | async-start | bytes 1081344 | tf_op jit(solution)/shard_map/reduce_scatter | solution.py:105
  780.9 472.1 %reduce-scatter.11.cloned.1.call-start = ((), (), s32[]{:S(2)}) async-start(), calls=%async_computation.7 | async-start | bytes 147456 | tf_op jit(solution)/shard_map/reduce_scatter | solution.py:121
Sparse Core Ops, SparseCore 0:
  12.5 55.0 all-gather.3
  199.6 33.6 reduce-scatter.4
  620.1 136.6 all-reduce.2
  779.6 218.4 reduce-scatter.8
  1002.3 215.2 reduce-scatter.6
  1220.5 32.4 reduce-scatter.10
